TPU v7x, 32 devices: a whole 2x2x4 slice. The times are simulated.
32 devices in a mesh: gx: 8 (over y, x, core), gy: 4 (over z).
Axes of the slice: x: 2, y: 2, z: 4, core: 2. Of those that a mesh axis runs over, the one named last changes fastest.
Arguments:
- probe_signs: int32 [32, 16, 64, 128], P(None, 'gx', 'gy'), may hold values from 0 to 1
- diagonal: float32 [16, 64, 128], P('gx', 'gy'), may hold values from 0.25 to 4
Outputs:
- diagonal_blocks: float32 [3, 32, 32], replicated
- offdiag_blocks: float32 [3, 32, 32], replicated
- next_block: float32 [32, 16, 64, 128], P(None, 'gx', 'gy')
All inputs are finite; a program needn't handle non-finite values.
Results may differ from a plain program's by a relative error of at most 0.0006.
Values sent between devices are 32-bit elements; how exact they have to be, the bound alone decides.
A program may use at most 64 MiB of HBM per device.

v0:
```python
import jax
import jax.numpy as jnp
from jax import lax
from jax.sharding import PartitionSpec as P

ITERS = 3


def with_halo(block, sides, width):
    for axis, dim in sides:
        count = lax.axis_size(axis)
        forward = [(i, i + 1) for i in range(count - 1)]
        forward.append((count - 1, 0))
        backward = [(target, source) for source, target in forward]
        low = lax.ppermute(
            lax.slice_in_dim(block, block.shape[dim] - width, None, axis=dim), axis, forward
        )
        high = lax.ppermute(lax.slice_in_dim(block, 0, width, axis=dim), axis, backward)
        block = jnp.concatenate([low, block, high], axis=dim)
    return block


def stencil(vectors, diagonal):
    padded = with_halo(vectors, (("gx", 1), ("gy", 2)), 1)
    beside = padded[:, 2:, 1:-1] + padded[:, :-2, 1:-1] + padded[:, 1:-1, 2:] + padded[:, 1:-1, :-2]
    beside = beside + jnp.roll(vectors, 1, 3) + jnp.roll(vectors, -1, 3)
    return (6.0 + diagonal)[None] * vectors - beside


def inner_block(left, right):
    return jnp.einsum("pxyz,qxyz->pq", left, right, precision=lax.Precision.HIGHEST)


def combine(vectors, matrix):
    return jnp.einsum("pxyz,pq->qxyz", vectors, matrix, precision=lax.Precision.HIGHEST)


def small_product(left, right):
    return jnp.dot(left, right, precision=lax.Precision.HIGHEST)


def inverse_lower(gram_matrix):
    lower_factor = jnp.linalg.cholesky(gram_matrix)
    identity_matrix = jnp.eye(gram_matrix.shape[0], dtype=gram_matrix.dtype)
    inverse = lax.linalg.triangular_solve(lower_factor, identity_matrix, left_side=True, lower=True)
    return (lower_factor, inverse)


def per_device(probe_signs, diagonal):
    total_cells = (
        probe_signs.shape[1]
        * lax.axis_size("gx")
        * probe_signs.shape[2]
        * lax.axis_size("gy")
        * probe_signs.shape[3]
    )
    scale_factor = 1.0 / jnp.sqrt(jnp.float32(total_cells))
    probes = (2.0 * probe_signs.astype(jnp.float32) - 1.0) * scale_factor
    probe_matrix = lax.psum(inner_block(probes, probes), ("gx", "gy"))
    lower_factor, inverse = inverse_lower(probe_matrix)
    current = combine(probes, inverse.T)
    previous = None
    coupling = None
    alphas = []
    betas = []
    for iteration in range(ITERS):
        image = stencil(current, diagonal)
        if previous is not None:
            image = image - combine(previous, coupling)
        projected, image_gram = lax.psum(
            (inner_block(current, image), inner_block(image, image)), ("gx", "gy")
        )
        remain = image - combine(current, projected)
        remain_gram = image_gram - small_product(projected.T, projected)
        lower_factor, inverse = inverse_lower(remain_gram)
        alphas.append(projected)
        betas.append(lower_factor.T)
        previous = current
        coupling = lower_factor
        current = combine(remain, inverse.T)
    return (jnp.stack(alphas), jnp.stack(betas), current)


def solution(mesh):
    in_specs = (P(None, "gx", "gy", None), P("gx", "gy", None))
    out_specs = (P(), P(), P(None, "gx", "gy", None))
    return jax.shard_map(
        per_device, mesh=mesh, in_specs=in_specs, out_specs=out_specs, check_vma=False
    )
```

profile of v0, /device:TPU:14, one launch (start us, length us, event | category | flops | bytes accessed | tf_op | source)
XLA Modules:
  0.0 253.6 jit_solution(12887706050572880338)
XLA Ops:
  2.6 40.3 %psum.49 = f32[32,32]{0,1:T(8,128)S(1)} all-reduce(f32[32,32]{0,1:T(8,128)S(1)} %convolution_bitcast_fusion.10), channel_id=1, replica_groups=mesh['gx'=8,'gy'=4] {'gx','gy'}, use_global_device_ids=true, to_apply=%region_0.0 | all-reduce | flops 1024 | bytes 8192 | tf_op jit(solution)/shard_map/psum | solution.py:59
  43.0 2.9 %cholesky.74 = f32[32,32]{1,0:T(8,128)S(1)} custom-call(f32[32,32]{1,0:T(8,128)S(1)} %fusion.38), custom_call_target="Cholesky" | custom-call | tf_op jit(solution)/shard_map/jit(cholesky)/cholesky | solution.py:43
  47.3 2.4 custom-call.8
  50.9 1.7 collective-permute-start
  53.1 3.7 %collective-permute-done.1 = f32[32,1,16,128]{3,0,2,1:T(8,128)S(1)} collective-permute-done((f32[32,1,16,128]{3,0,2,1:T(8,128)S(1)}, f32[32,1,16,128]{3,0,2,1:T(8,128)S(1)}, u32[]{:S(2)}, u32[]{:S(2)}) %collective-permute-start.1) | collective-permute-done | bytes 262176 | tf_op jit(solution)/shard_map/ppermute | solution.py:15
  59.8 2.2 collective-permute-done.2
  65.0 44.6 %all-reduce.2 = (f32[32,32]{0,1:T(8,128)S(1)}, f32[32,32]{1,0:T(8,128)S(1)}) all-reduce(f32[32,32]{0,1:T(8,128)S(1)} %convolution_bitcast_fusion.7, f32[32,32]{1,0:T(8,128)S(1)} %convolution_bitcast_fusion.8), channel_id=1, replica_groups=mesh['gx'=8,'gy'=4] {'gx','gy'}, use_global_device_ids=true, to_apply=%region_4.7 | all-reduce | flops 2048 | bytes 16384 | tf_op jit(solution)/shard_map/psum | solution.py:70
  110.5 2.9 %cholesky.85 = f32[32,32]{1,0:T(8,128)S(1)} custom-call(f32[32,32]{1,0:T(8,128)S(1)} %fusion.36), custom_call_target="Cholesky" | custom-call | tf_op jit(solution)/shard_map/jit(cholesky)/cholesky | solution.py:43
  114.8 2.4 custom-call.9
  118.2 1.7 collective-permute-start.4
  120.1 5.4 %collective-permute-done.5 = f32[32,1,16,128]{3,0,2,1:T(8,128)S(1)} collective-permute-done((f32[32,1,16,128]{3,0,2,1:T(8,128)S(1)}, f32[32,1,16,128]{3,0,2,1:T(8,128)S(1)}, u32[]{:S(2)}, u32[]{:S(2)}) %collective-permute-start.5) | collective-permute-done | bytes 262176 | tf_op jit(solution)/shard_map/ppermute | solution.py:15
  125.6 2.0 collective-permute-start.7
  127.8 2.2 collective-permute-done.6
  130.9 1.6 convolution_subtract_fusion.3
  133.6 42.3 %all-reduce.1 = (f32[32,32]{0,1:T(8,128)S(1)}, f32[32,32]{1,0:T(8,128)S(1)}) all-reduce(f32[32,32]{0,1:T(8,128)S(1)} %convolution_bitcast_fusion.4, f32[32,32]{1,0:T(8,128)S(1)} %convolution_bitcast_fusion.5), channel_id=1, replica_groups=mesh['gx'=8,'gy'=4] {'gx','gy'}, use_global_device_ids=true, to_apply=%region_6.9 | all-reduce | flops 2048 | bytes 16384 | tf_op jit(solution)/shard_map/psum | solution.py:70
  176.8 2.9 %cholesky.96 = f32[32,32]{1,0:T(8,128)S(1)} custom-call(f32[32,32]{1,0:T(8,128)S(1)} %fusion.33), custom_call_target="Cholesky" | custom-call | tf_op jit(solution)/shard_map/jit(cholesky)/cholesky | solution.py:43
  181.1 2.4 custom-call.10
  184.4 1.7 collective-permute-start.8
  186.4 4.8 %collective-permute-done.9 = f32[32,1,16,128]{3,0,2,1:T(8,128)S(1)} collective-permute-done((f32[32,1,16,128]{3,0,2,1:T(8,128)S(1)}, f32[32,1,16,128]{3,0,2,1:T(8,128)S(1)}, u32[]{:S(2)}, u32[]{:S(2)}) %collective-permute-start.9) | collective-permute-done | bytes 262176 | tf_op jit(solution)/shard_map/ppermute | solution.py:15
  191.3 2.0 collective-permute-start.11
  193.5 2.0 collective-permute-done.10
  198.7 44.0 %all-reduce = (f32[32,32]{1,0:T(8,128)S(1)}, f32[32,32]{0,1:T(8,128)S(1)}) all-reduce(f32[32,32]{1,0:T(8,128)S(1)} %convolution_bitcast_fusion.2, f32[32,32]{0,1:T(8,128)S(1)} %convolution_bitcast_fusion.1), channel_id=1, replica_groups=mesh['gx'=8,'gy'=4] {'gx','gy'}, use_global_device_ids=true, to_apply=%region_7.10 | all-reduce | flops 2048 | bytes 16384 | tf_op jit(solution)/shard_map/psum | solution.py:70
  243.6 2.9 %cholesky.107 = f32[32,32]{1,0:T(8,128)S(1)} custom-call(f32[32,32]{1,0:T(8,128)S(1)} %fusion.30), custom_call_target="Cholesky" | custom-call | tf_op jit(solution)/shard_map/jit(cholesky)/cholesky | solution.py:43
  247.9 2.4 custom-call.11
  (76 shorter events, 28.6 us)
Async XLA Ops:
  50.9 6.0 %collective-permute-start.1 = (f32[32,1,16,128]{3,0,2,1:T(8,128)S(1)}, f32[32,1,16,128]{3,0,2,1:T(8,128)S(1)}, u32[]{:S(2)}, u32[]{:S(2)}) collective-permute-start(f32[32,1,16,128]{3,0,2,1:T(8,128)S(1)} %get-tuple-element.36), channel_id=1, source_target_pairs={{0,4},{4,8},{8,12},{12,16},{16,20},{20,24},{24,28},{28,0},{1,5},{5... | collective-permute-start | bytes 786440 | tf_op jit(solution)/shard_map/ppermute | solution.py:15
  50.9 6.8 %collective-permute-start = (f32[32,1,16,128]{3,0,2,1:T(8,128)S(1)}, f32[32,1,16,128]{3,0,2,1:T(8,128)S(1)}, u32[]{:S(2)}, u32[]{:S(2)}) collective-permute-start(f32[32,1,16,128]{3,0,2,1:T(8,128)S(1)} %get-tuple-element.37), channel_id=1, source_target_pairs={{4,0},{8,4},{12,8},{16,12},{20,16},{24,20},{28,24},{0,28},{5,1},{9... | collective-permute-start | bytes 786440 | tf_op jit(solution)/shard_map/ppermute | solution.py:18
  53.1 6.7 %copy-start = (f32[2,16,128]{2,1,0:T(8,128)S(1)}, f32[2,16,128]{2,1,0:T(8,128)}, u32[]{:S(2)}) copy-start(f32[2,16,128]{2,1,0:T(8,128)} %param.6) | copy-start | bytes 49156
  57.7 4.3 %collective-permute-start.2 = (f32[32,4,1,128]{3,0,2,1:T(8,128)S(1)}, f32[32,4,1,128]{3,0,2,1:T(8,128)S(1)}, u32[]{:S(2)}, u32[]{:S(2)}) collective-permute-start(f32[32,4,1,128]{3,0,2,1:T(8,128)S(1)} %get-tuple-element.18), channel_id=1, source_target_pairs={{1,0},{2,1},{3,2},{0,3},{5,4},{6,5},{7,6},{4,7},{9,8},{10,9},{11,1... | collective-permute-start | bytes 196616 | tf_op jit(solution)/shard_map/ppermute | solution.py:18
  58.3 5.1 %collective-permute-start.3 = (f32[32,4,1,128]{3,0,2,1:T(8,128)S(1)}, f32[32,4,1,128]{3,0,2,1:T(8,128)S(1)}, u32[]{:S(2)}, u32[]{:S(2)}) collective-permute-start(f32[32,4,1,128]{3,0,2,1:T(8,128)S(1)} %get-tuple-element.19), channel_id=1, source_target_pairs={{0,1},{1,2},{2,3},{3,0},{4,5},{5,6},{6,7},{7,4},{8,9},{9,10},{10,1... | collective-permute-start | bytes 196616 | tf_op jit(solution)/shard_map/ppermute | solution.py:15
  118.1 7.4 %collective-permute-start.5 = (f32[32,1,16,128]{3,0,2,1:T(8,128)S(1)}, f32[32,1,16,128]{3,0,2,1:T(8,128)S(1)}, u32[]{:S(2)}, u32[]{:S(2)}) collective-permute-start(f32[32,1,16,128]{3,0,2,1:T(8,128)S(1)} %get-tuple-element.30), channel_id=1, source_target_pairs={{0,4},{4,8},{8,12},{12,16},{16,20},{20,24},{24,28},{28,0},{1,5},{5... | collective-permute-start | bytes 786440 | tf_op jit(solution)/shard_map/ppermute | solution.py:15
  118.2 7.4 %collective-permute-start.4 = (f32[32,1,16,128]{3,0,2,1:T(8,128)S(1)}, f32[32,1,16,128]{3,0,2,1:T(8,128)S(1)}, u32[]{:S(2)}, u32[]{:S(2)}) collective-permute-start(f32[32,1,16,128]{3,0,2,1:T(8,128)S(1)} %get-tuple-element.31), channel_id=1, source_target_pairs={{4,0},{8,4},{12,8},{16,12},{20,16},{24,20},{28,24},{0,28},{5,1},{9... | collective-permute-start | bytes 786440 | tf_op jit(solution)/shard_map/ppermute | solution.py:18
  125.5 4.5 %collective-permute-start.6 = (f32[32,4,1,128]{3,0,2,1:T(8,128)S(1)}, f32[32,4,1,128]{3,0,2,1:T(8,128)S(1)}, u32[]{:S(2)}, u32[]{:S(2)}) collective-permute-start(f32[32,4,1,128]{3,0,2,1:T(8,128)S(1)} %get-tuple-element.16), channel_id=1, source_target_pairs={{1,0},{2,1},{3,2},{0,3},{5,4},{6,5},{7,6},{4,7},{9,8},{10,9},{11,1... | collective-permute-start | bytes 196616 | tf_op jit(solution)/shard_map/ppermute | solution.py:18
  125.6 5.3 %collective-permute-start.7 = (f32[32,4,1,128]{3,0,2,1:T(8,128)S(1)}, f32[32,4,1,128]{3,0,2,1:T(8,128)S(1)}, u32[]{:S(2)}, u32[]{:S(2)}) collective-permute-start(f32[32,4,1,128]{3,0,2,1:T(8,128)S(1)} %get-tuple-element.17), channel_id=1, source_target_pairs={{0,1},{1,2},{2,3},{3,0},{4,5},{5,6},{6,7},{7,4},{8,9},{9,10},{10,1... | collective-permute-start | bytes 196616 | tf_op jit(solution)/shard_map/ppermute | solution.py:15
  184.4 6.8 %collective-permute-start.9 = (f32[32,1,16,128]{3,0,2,1:T(8,128)S(1)}, f32[32,1,16,128]{3,0,2,1:T(8,128)S(1)}, u32[]{:S(2)}, u32[]{:S(2)}) collective-permute-start(f32[32,1,16,128]{3,0,2,1:T(8,128)S(1)} %get-tuple-element.24), channel_id=1, source_target_pairs={{0,4},{4,8},{8,12},{12,16},{16,20},{20,24},{24,28},{28,0},{1,5},{5... | collective-permute-start | bytes 786440 | tf_op jit(solution)/shard_map/ppermute | solution.py:15
  184.4 6.8 %collective-permute-start.8 = (f32[32,1,16,128]{3,0,2,1:T(8,128)S(1)}, f32[32,1,16,128]{3,0,2,1:T(8,128)S(1)}, u32[]{:S(2)}, u32[]{:S(2)}) collective-permute-start(f32[32,1,16,128]{3,0,2,1:T(8,128)S(1)} %get-tuple-element.25), channel_id=1, source_target_pairs={{4,0},{8,4},{12,8},{16,12},{20,16},{24,20},{28,24},{0,28},{5,1},{9... | collective-permute-start | bytes 786440 | tf_op jit(solution)/shard_map/ppermute | solution.py:18
  191.2 4.3 %collective-permute-start.10 = (f32[32,4,1,128]{3,0,2,1:T(8,128)S(1)}, f32[32,4,1,128]{3,0,2,1:T(8,128)S(1)}, u32[]{:S(2)}, u32[]{:S(2)}) collective-permute-start(f32[32,4,1,128]{3,0,2,1:T(8,128)S(1)} %get-tuple-element.14), channel_id=1, source_target_pairs={{1,0},{2,1},{3,2},{0,3},{5,4},{6,5},{7,6},{4,7},{9,8},{10,9},{11,1... | collective-permute-start | bytes 196616 | tf_op jit(solution)/shard_map/ppermute | solution.py:18
  191.3 4.8 %collective-permute-start.11 = (f32[32,4,1,128]{3,0,2,1:T(8,128)S(1)}, f32[32,4,1,128]{3,0,2,1:T(8,128)S(1)}, u32[]{:S(2)}, u32[]{:S(2)}) collective-permute-start(f32[32,4,1,128]{3,0,2,1:T(8,128)S(1)} %get-tuple-element.15), channel_id=1, source_target_pairs={{0,1},{1,2},{2,3},{3,0},{4,5},{5,6},{6,7},{7,4},{8,9},{9,10},{10,1... | collective-permute-start | bytes 196616 | tf_op jit(solution)/shard_map/ppermute | solution.py:15
where the time goes:
time: 254 us
  blocking collectives  171 us (67%)
  other arithmetic  28.9 us (11%)
  waiting for transfers between devices  24.1 us (9%)
  matrix products  13.3 us (5%)
  starting transfers between devices  11.6 us (5%)
  local copies, waits for them, and re-layouts  3.44 us (1%)
    psum x3, blocking collectives, per_device(): lax.psum((inner_block(current, image), inner_block(image, image)), ('gx',...  131 us
    psum x1, blocking collectives, per_device(): probe_matrix = lax.psum(inner_block(probes, probes), ('gx', 'gy'))  40.3 us
    ppermute x6, waiting for transfers between devices, with_halo(): lax.ppermute(lax.slice_in_dim(block, block.shape[dim] - width, None, axis...  16.7 us
    another operation x12, other arithmetic, inverse_lower(): lower_factor = jnp.linalg.cholesky(gram_matrix)  14.4 us
    another operation x6, other arithmetic, inverse_lower(): lax.linalg.triangular_solve(lower_factor, identity_matrix, left_side=True...  11 us
    dot_general x9, matrix products, combine(): jnp.einsum('pxyz,pq->qxyz', vectors, matrix, precision=lax.Precision.HIGH...  7.62 us
    ppermute x6, waiting for transfers between devices, with_halo(): lax.ppermute(lax.slice_in_dim(block, 0, width, axis=dim), axis, backward)  7.37 us
    ppermute x6, starting transfers between devices, with_halo(): lax.ppermute(lax.slice_in_dim(block, 0, width, axis=dim), axis, backward)  5.89 us
  transfers between devices with their start and end apart: 12, of which 10 were waited for; matrix products, arithmetic and copies ran while one was open for 0% of the time, Pallas kernels for 0%

commit v1 on v0

--- a/solution.py
+++ b/solution.py
@@ -68,7 +68,7 @@
         if previous is not None:
             image = image - combine(previous, coupling)
         projected, image_gram = lax.psum(
-            (inner_block(current, image), inner_block(image, image)), ("gx", "gy")
+            lax.psum((inner_block(current, image), inner_block(image, image)), "gy"), "gx"
         )
         remain = image - combine(current, projected)
         remain_gram = image_gram - small_product(projected.T, projected)

time: 254 us -> 253 us (level)
  the two profiles are of different devices: /device:TPU:14 before, /device:TPU:0 now
where the time goes in v1:
time: 253 us
  blocking collectives  158 us (62%)
  waiting for transfers between devices  33.4 us (13%)
  other arithmetic  28.9 us (11%)
  starting transfers between devices  14.5 us (6%)
  matrix products  13.3 us (5%)
  local copies, waits for them, and re-layouts  3.44 us (1%)
    psum x3, blocking collectives, per_device(): lax.psum(lax.psum((inner_block(current, image), inner_block(image, image)...  67.3 us
    psum x3, blocking collectives, per_device(): lax.psum((inner_block(current, image), inner_block(image, image)), 'gy')  48.7 us
    psum x1, blocking collectives, per_device(): probe_matrix = lax.psum(inner_block(probes, probes), ('gx', 'gy'))  42.1 us
    ppermute x6, waiting for transfers between devices, with_halo(): lax.ppermute(lax.slice_in_dim(block, block.shape[dim] - width, None, axis...  26.4 us
    another operation x12, other arithmetic, inverse_lower(): lower_factor = jnp.linalg.cholesky(gram_matrix)  14.4 us
    ppermute x6, starting transfers between devices, with_halo(): lax.ppermute(lax.slice_in_dim(block, 0, width, axis=dim), axis, backward)  13.1 us
    another operation x6, other arithmetic, inverse_lower(): lax.linalg.triangular_solve(lower_factor, identity_matrix, left_side=True...  11 us
    dot_general x9, matrix products, combine(): jnp.einsum('pxyz,pq->qxyz', vectors, matrix, precision=lax.Precision.HIGH...  7.63 us
  transfers between devices with their start and end apart: 12, of which 10 were waited for; matrix products, arithmetic and copies ran while one was open for 0% of the time, Pallas kernels for 0%

profile of v1, /device:TPU:0, one launch (start us, length us, event | category | flops | bytes accessed | tf_op | source)
XLA Modules:
  0.0 252.7 jit_solution(17278032566777681876)
XLA Ops:
  2.6 42.1 %psum.91 = f32[32,32]{0,1:T(8,128)S(1)} all-reduce(f32[32,32]{0,1:T(8,128)S(1)} %convolution_bitcast_fusion.10), channel_id=1, replica_groups=mesh['gx'=8,'gy'=4] {'gx','gy'}, use_global_device_ids=true, to_apply=%region_0.0 | all-reduce | flops 1024 | bytes 8192 | tf_op jit(solution)/shard_map/psum | solution.py:59
  44.7 2.9 %cholesky.74 = f32[32,32]{1,0:T(8,128)S(1)} custom-call(f32[32,32]{1,0:T(8,128)S(1)} %fusion.38), custom_call_target="Cholesky" | custom-call | tf_op jit(solution)/shard_map/jit(cholesky)/cholesky | solution.py:43
  49.0 2.4 custom-call.8
  52.7 2.6 %collective-permute-start = (f32[32,1,16,128]{3,0,2,1:T(8,128)S(1)}, f32[32,1,16,128]{3,0,2,1:T(8,128)S(1)}, u32[]{:S(2)}, u32[]{:S(2)}) collective-permute-start(f32[32,1,16,128]{3,0,2,1:T(8,128)S(1)} %get-tuple-element.43), channel_id=1, source_target_pairs={{4,0},{8,4},{12,8},{16,12},{20,16},{24,20},{28,24},{0,28},{5,1},{9... | collective-permute-start | bytes 786440 | tf_op jit(solution)/shard_map/ppermute | solution.py:18
  55.7 4.8 %collective-permute-done.1 = f32[32,1,16,128]{3,0,2,1:T(8,128)S(1)} collective-permute-done((f32[32,1,16,128]{3,0,2,1:T(8,128)S(1)}, f32[32,1,16,128]{3,0,2,1:T(8,128)S(1)}, u32[]{:S(2)}, u32[]{:S(2)}) %collective-permute-start.1) | collective-permute-done | bytes 262176 | tf_op jit(solution)/shard_map/ppermute | solution.py:15
  65.4 4.2 %collective-permute-done.3 = f32[32,4,1,128]{3,0,2,1:T(8,128)S(1)} collective-permute-done((f32[32,4,1,128]{3,0,2,1:T(8,128)S(1)}, f32[32,4,1,128]{3,0,2,1:T(8,128)S(1)}, u32[]{:S(2)}, u32[]{:S(2)}) %collective-permute-start.3) | collective-permute-done | bytes 65568 | tf_op jit(solution)/shard_map/ppermute | solution.py:15
  71.1 17.1 %all-reduce.5 = (f32[32,32]{0,1:T(8,128)S(1)}, f32[32,32]{1,0:T(8,128)S(1)}) all-reduce(f32[32,32]{0,1:T(8,128)S(1)} %convolution_bitcast_fusion.7, f32[32,32]{1,0:T(8,128)S(1)} %convolution_bitcast_fusion.8), channel_id=1, replica_groups=mesh['gx'=8,'gy'=4] {'gy'}, use_global_device_ids=true, to_apply=%region_5.8 | all-reduce | flops 2048 | bytes 16384 | tf_op jit(solution)/shard_map/psum | solution.py:71
  88.2 22.4 %all-reduce.2 = (f32[32,32]{0,1:T(8,128)S(1)}, f32[32,32]{1,0:T(8,128)S(1)}) all-reduce(f32[32,32]{0,1:T(8,128)S(1)} %get-tuple-element.18, f32[32,32]{1,0:T(8,128)S(1)} %get-tuple-element.19), channel_id=1, replica_groups=mesh['gx'=8,'gy'=4] {'gx'}, use_global_device_ids=true, to_apply=%region_6.9 | all-reduce | flops 2048 | bytes 16384 | tf_op jit(solution)/shard_map/psum | solution.py:70
  111.5 2.9 %cholesky.85 = f32[32,32]{1,0:T(8,128)S(1)} custom-call(f32[32,32]{1,0:T(8,128)S(1)} %fusion.36), custom_call_target="Cholesky" | custom-call | tf_op jit(solution)/shard_map/jit(cholesky)/cholesky | solution.py:43
  115.8 2.4 custom-call.9
  119.2 2.6 %collective-permute-start.4 = (f32[32,1,16,128]{3,0,2,1:T(8,128)S(1)}, f32[32,1,16,128]{3,0,2,1:T(8,128)S(1)}, u32[]{:S(2)}, u32[]{:S(2)}) collective-permute-start(f32[32,1,16,128]{3,0,2,1:T(8,128)S(1)} %get-tuple-element.37), channel_id=1, source_target_pairs={{4,0},{8,4},{12,8},{16,12},{20,16},{24,20},{28,24},{0,28},{5,1},{9... | collective-permute-start | bytes 786440 | tf_op jit(solution)/shard_map/ppermute | solution.py:18
  122.0 5.8 %collective-permute-done.5 = f32[32,1,16,128]{3,0,2,1:T(8,128)S(1)} collective-permute-done((f32[32,1,16,128]{3,0,2,1:T(8,128)S(1)}, f32[32,1,16,128]{3,0,2,1:T(8,128)S(1)}, u32[]{:S(2)}, u32[]{:S(2)}) %collective-permute-start.5) | collective-permute-done | bytes 262176 | tf_op jit(solution)/shard_map/ppermute | solution.py:15
  132.5 2.8 %collective-permute-done.7 = f32[32,4,1,128]{3,0,2,1:T(8,128)S(1)} collective-permute-done((f32[32,4,1,128]{3,0,2,1:T(8,128)S(1)}, f32[32,4,1,128]{3,0,2,1:T(8,128)S(1)}, u32[]{:S(2)}, u32[]{:S(2)}) %collective-permute-start.7) | collective-permute-done | bytes 65568 | tf_op jit(solution)/shard_map/ppermute | solution.py:15
  137.9 15.8 %all-reduce.4 = (f32[32,32]{0,1:T(8,128)S(1)}, f32[32,32]{1,0:T(8,128)S(1)}) all-reduce(f32[32,32]{0,1:T(8,128)S(1)} %convolution_bitcast_fusion.4, f32[32,32]{1,0:T(8,128)S(1)} %convolution_bitcast_fusion.5), channel_id=1, replica_groups=mesh['gx'=8,'gy'=4] {'gy'}, use_global_device_ids=true, to_apply=%region_9.12 | all-reduce | flops 2048 | bytes 16384 | tf_op jit(solution)/shard_map/psum | solution.py:71
  153.7 22.6 %all-reduce.1 = (f32[32,32]{0,1:T(8,128)S(1)}, f32[32,32]{1,0:T(8,128)S(1)}) all-reduce(f32[32,32]{0,1:T(8,128)S(1)} %get-tuple-element.16, f32[32,32]{1,0:T(8,128)S(1)} %get-tuple-element.17), channel_id=1, replica_groups=mesh['gx'=8,'gy'=4] {'gx'}, use_global_device_ids=true, to_apply=%region_10.13 | all-reduce | flops 2048 | bytes 16384 | tf_op jit(solution)/shard_map/psum | solution.py:70
  177.2 2.9 %cholesky.96 = f32[32,32]{1,0:T(8,128)S(1)} custom-call(f32[32,32]{1,0:T(8,128)S(1)} %fusion.33), custom_call_target="Cholesky" | custom-call | tf_op jit(solution)/shard_map/jit(cholesky)/cholesky | solution.py:43
  181.5 2.4 custom-call.10
  184.9 2.6 %collective-permute-start.8 = (f32[32,1,16,128]{3,0,2,1:T(8,128)S(1)}, f32[32,1,16,128]{3,0,2,1:T(8,128)S(1)}, u32[]{:S(2)}, u32[]{:S(2)}) collective-permute-start(f32[32,1,16,128]{3,0,2,1:T(8,128)S(1)} %get-tuple-element.31), channel_id=1, source_target_pairs={{4,0},{8,4},{12,8},{16,12},{20,16},{24,20},{28,24},{0,28},{5,1},{9... | collective-permute-start | bytes 786440 | tf_op jit(solution)/shard_map/ppermute | solution.py:18
  187.7 5.4 %collective-permute-done.9 = f32[32,1,16,128]{3,0,2,1:T(8,128)S(1)} collective-permute-done((f32[32,1,16,128]{3,0,2,1:T(8,128)S(1)}, f32[32,1,16,128]{3,0,2,1:T(8,128)S(1)}, u32[]{:S(2)}, u32[]{:S(2)}) %collective-permute-start.9) | collective-permute-done | bytes 262176 | tf_op jit(solution)/shard_map/ppermute | solution.py:15
  197.5 3.4 %collective-permute-done.11 = f32[32,4,1,128]{3,0,2,1:T(8,128)S(1)} collective-permute-done((f32[32,4,1,128]{3,0,2,1:T(8,128)S(1)}, f32[32,4,1,128]{3,0,2,1:T(8,128)S(1)}, u32[]{:S(2)}, u32[]{:S(2)}) %collective-permute-start.11) | collective-permute-done | bytes 65568 | tf_op jit(solution)/shard_map/ppermute | solution.py:15
  203.6 15.8 %all-reduce.3 = (f32[32,32]{1,0:T(8,128)S(1)}, f32[32,32]{0,1:T(8,128)S(1)}) all-reduce(f32[32,32]{1,0:T(8,128)S(1)} %convolution_bitcast_fusion.2, f32[32,32]{0,1:T(8,128)S(1)} %convolution_bitcast_fusion.1), channel_id=1, replica_groups=mesh['gx'=8,'gy'=4] {'gy'}, use_global_device_ids=true, to_apply=%region_11.14 | all-reduce | flops 2048 | bytes 16384 | tf_op jit(solution)/shard_map/psum | solution.py:71
  219.4 22.4 %all-reduce = (f32[32,32]{1,0:T(8,128)S(1)}, f32[32,32]{0,1:T(8,128)S(1)}) all-reduce(f32[32,32]{1,0:T(8,128)S(1)} %get-tuple-element.14, f32[32,32]{0,1:T(8,128)S(1)} %get-tuple-element.15), channel_id=1, replica_groups=mesh['gx'=8,'gy'=4] {'gx'}, use_global_device_ids=true, to_apply=%region_12.15 | all-reduce | flops 2048 | bytes 16384 | tf_op jit(solution)/shard_map/psum | solution.py:70
  242.7 2.9 %cholesky.107 = f32[32,32]{1,0:T(8,128)S(1)} custom-call(f32[32,32]{1,0:T(8,128)S(1)} %fusion.30), custom_call_target="Cholesky" | custom-call | tf_op jit(solution)/shard_map/jit(cholesky)/cholesky | solution.py:43
  247.0 2.4 custom-call.11
  (79 shorter events, 37.8 us)
Async XLA Ops:
  52.6 7.9 %collective-permute-start.1 = (f32[32,1,16,128]{3,0,2,1:T(8,128)S(1)}, f32[32,1,16,128]{3,0,2,1:T(8,128)S(1)}, u32[]{:S(2)}, u32[]{:S(2)}) collective-permute-start(f32[32,1,16,128]{3,0,2,1:T(8,128)S(1)} %get-tuple-element.42), channel_id=1, source_target_pairs={{0,4},{4,8},{8,12},{12,16},{16,20},{20,24},{24,28},{28,0},{1,5},{5... | collective-permute-start | bytes 786440 | tf_op jit(solution)/shard_map/ppermute | solution.py:15
  52.7 8.4 %collective-permute-start = (f32[32,1,16,128]{3,0,2,1:T(8,128)S(1)}, f32[32,1,16,128]{3,0,2,1:T(8,128)S(1)}, u32[]{:S(2)}, u32[]{:S(2)}) collective-permute-start(f32[32,1,16,128]{3,0,2,1:T(8,128)S(1)} %get-tuple-element.43), channel_id=1, source_target_pairs={{4,0},{8,4},{12,8},{16,12},{20,16},{24,20},{28,24},{0,28},{5,1},{9... | collective-permute-start | bytes 786440 | tf_op jit(solution)/shard_map/ppermute | solution.py:18
  55.7 7.6 %copy-start = (f32[2,16,128]{2,1,0:T(8,128)S(1)}, f32[2,16,128]{2,1,0:T(8,128)}, u32[]{:S(2)}) copy-start(f32[2,16,128]{2,1,0:T(8,128)} %param.6) | copy-start | bytes 49156
  61.1 4.3 %collective-permute-start.2 = (f32[32,4,1,128]{3,0,2,1:T(8,128)S(1)}, f32[32,4,1,128]{3,0,2,1:T(8,128)S(1)}, u32[]{:S(2)}, u32[]{:S(2)}) collective-permute-start(f32[32,4,1,128]{3,0,2,1:T(8,128)S(1)} %get-tuple-element.24), channel_id=1, source_target_pairs={{1,0},{2,1},{3,2},{0,3},{5,4},{6,5},{7,6},{4,7},{9,8},{10,9},{11,1... | collective-permute-start | bytes 196616 | tf_op jit(solution)/shard_map/ppermute | solution.py:18
  63.3 6.2 %collective-permute-start.3 = (f32[32,4,1,128]{3,0,2,1:T(8,128)S(1)}, f32[32,4,1,128]{3,0,2,1:T(8,128)S(1)}, u32[]{:S(2)}, u32[]{:S(2)}) collective-permute-start(f32[32,4,1,128]{3,0,2,1:T(8,128)S(1)} %get-tuple-element.25), channel_id=1, source_target_pairs={{0,1},{1,2},{2,3},{3,0},{4,5},{5,6},{6,7},{7,4},{8,9},{9,10},{10,1... | collective-permute-start | bytes 196616 | tf_op jit(solution)/shard_map/ppermute | solution.py:15
  119.1 8.7 %collective-permute-start.5 = (f32[32,1,16,128]{3,0,2,1:T(8,128)S(1)}, f32[32,1,16,128]{3,0,2,1:T(8,128)S(1)}, u32[]{:S(2)}, u32[]{:S(2)}) collective-permute-start(f32[32,1,16,128]{3,0,2,1:T(8,128)S(1)} %get-tuple-element.36), channel_id=1, source_target_pairs={{0,4},{4,8},{8,12},{12,16},{16,20},{20,24},{24,28},{28,0},{1,5},{5... | collective-permute-start | bytes 786440 | tf_op jit(solution)/shard_map/ppermute | solution.py:15
  119.2 8.7 %collective-permute-start.4 = (f32[32,1,16,128]{3,0,2,1:T(8,128)S(1)}, f32[32,1,16,128]{3,0,2,1:T(8,128)S(1)}, u32[]{:S(2)}, u32[]{:S(2)}) collective-permute-start(f32[32,1,16,128]{3,0,2,1:T(8,128)S(1)} %get-tuple-element.37), channel_id=1, source_target_pairs={{4,0},{8,4},{12,8},{16,12},{20,16},{24,20},{28,24},{0,28},{5,1},{9... | collective-permute-start | bytes 786440 | tf_op jit(solution)/shard_map/ppermute | solution.py:18
  127.8 4.6 %collective-permute-start.6 = (f32[32,4,1,128]{3,0,2,1:T(8,128)S(1)}, f32[32,4,1,128]{3,0,2,1:T(8,128)S(1)}, u32[]{:S(2)}, u32[]{:S(2)}) collective-permute-start(f32[32,4,1,128]{3,0,2,1:T(8,128)S(1)} %get-tuple-element.22), channel_id=1, source_target_pairs={{1,0},{2,1},{3,2},{0,3},{5,4},{6,5},{7,6},{4,7},{9,8},{10,9},{11,1... | collective-permute-start | bytes 196616 | tf_op jit(solution)/shard_map/ppermute | solution.py:18
  129.2 6.1 %collective-permute-start.7 = (f32[32,4,1,128]{3,0,2,1:T(8,128)S(1)}, f32[32,4,1,128]{3,0,2,1:T(8,128)S(1)}, u32[]{:S(2)}, u32[]{:S(2)}) collective-permute-start(f32[32,4,1,128]{3,0,2,1:T(8,128)S(1)} %get-tuple-element.23), channel_id=1, source_target_pairs={{0,1},{1,2},{2,3},{3,0},{4,5},{5,6},{6,7},{7,4},{8,9},{9,10},{10,1... | collective-permute-start | bytes 196616 | tf_op jit(solution)/shard_map/ppermute | solution.py:15
  184.8 8.3 %collective-permute-start.9 = (f32[32,1,16,128]{3,0,2,1:T(8,128)S(1)}, f32[32,1,16,128]{3,0,2,1:T(8,128)S(1)}, u32[]{:S(2)}, u32[]{:S(2)}) collective-permute-start(f32[32,1,16,128]{3,0,2,1:T(8,128)S(1)} %get-tuple-element.30), channel_id=1, source_target_pairs={{0,4},{4,8},{8,12},{12,16},{16,20},{20,24},{24,28},{28,0},{1,5},{5... | collective-permute-start | bytes 786440 | tf_op jit(solution)/shard_map/ppermute | solution.py:15
  184.9 8.3 %collective-permute-start.8 = (f32[32,1,16,128]{3,0,2,1:T(8,128)S(1)}, f32[32,1,16,128]{3,0,2,1:T(8,128)S(1)}, u32[]{:S(2)}, u32[]{:S(2)}) collective-permute-start(f32[32,1,16,128]{3,0,2,1:T(8,128)S(1)} %get-tuple-element.31), channel_id=1, source_target_pairs={{4,0},{8,4},{12,8},{16,12},{20,16},{24,20},{28,24},{0,28},{5,1},{9... | collective-permute-start | bytes 786440 | tf_op jit(solution)/shard_map/ppermute | solution.py:18
  193.1 4.3 %collective-permute-start.10 = (f32[32,4,1,128]{3,0,2,1:T(8,128)S(1)}, f32[32,4,1,128]{3,0,2,1:T(8,128)S(1)}, u32[]{:S(2)}, u32[]{:S(2)}) collective-permute-start(f32[32,4,1,128]{3,0,2,1:T(8,128)S(1)} %get-tuple-element.20), channel_id=1, source_target_pairs={{1,0},{2,1},{3,2},{0,3},{5,4},{6,5},{7,6},{4,7},{9,8},{10,9},{11,1... | collective-permute-start | bytes 196616 | tf_op jit(solution)/shard_map/ppermute | solution.py:18
  194.8 6.1 %collective-permute-start.11 = (f32[32,4,1,128]{3,0,2,1:T(8,128)S(1)}, f32[32,4,1,128]{3,0,2,1:T(8,128)S(1)}, u32[]{:S(2)}, u32[]{:S(2)}) collective-permute-start(f32[32,4,1,128]{3,0,2,1:T(8,128)S(1)} %get-tuple-element.21), channel_id=1, source_target_pairs={{0,1},{1,2},{2,3},{3,0},{4,5},{5,6},{6,7},{7,4},{8,9},{9,10},{10,1... | collective-permute-start | bytes 196616 | tf_op jit(solution)/shard_map/ppermute | solution.py:15
